TPU v7x, 256 devices: a whole 4x4x8 slice. The times are simulated.
256 devices in a mesh: pair: 64 (over z, x, y_lo), mo: 4 (over y_hi, core).
Axes of the slice: x: 4, y: 4 (y_hi: 2, y_lo: 2; y = y_hi * 2 + y_lo), z: 8, core: 2. Of those that a mesh axis runs over, the one named last changes fastest.
Arguments:
- integrals: bfloat16 [1024, 1000, 1000], P('pair', 'mo'), may hold values from -6 to 6
- coeffs: bfloat16 [1000, 512], replicated, may hold values from -0.1875 to 0.1875
- mirror: int32 [1024], replicated, may hold values from 0 to 1023, as said below
Outputs:
- combined: float32 [1024, 512, 512], P(None, 'pair', 'mo')
Inputs may be any that keep to these rules, and one draw needn't show every extreme that they name: mirror pairs the rows: mirror[mirror[k]] = k and mirror[k] != k for every row k; a row and its mirror may lie on any devices.
All inputs are finite; a program needn't handle non-finite values.
Results may differ from a plain program's by a relative error of at most 0.0029.
Values may be sent and summed in bfloat16 or wider, within the bound.
A program may use at most 128 MiB of HBM per device.

v0:
```python
import jax
import jax.numpy as jnp
from jax import lax
from jax.sharding import PartitionSpec as P


def on_device(integrals, coeffs, mirror):
    quarter = jnp.einsum(
        "krs,sj->krj", integrals, coeffs, preferred_element_type=jnp.float32
    ).astype(jnp.bfloat16)
    arrived = lax.all_to_all(quarter, "mo", split_axis=2, concat_axis=1, tiled=True)
    half = jnp.einsum("ri,krj->kij", coeffs, arrived, preferred_element_type=jnp.float32)
    pieces = lax.all_to_all(half, "pair", split_axis=1, concat_axis=0, tiled=True)
    partner = jnp.take(pieces, mirror, axis=0)
    return 0.5 * (pieces + partner)


def solution(mesh):
    return jax.shard_map(
        on_device,
        mesh=mesh,
        in_specs=(P("pair", "mo", None), P(), P()),
        out_specs=P(None, "pair", "mo"),
        check_vma=False,
    )
```

profile of v0, /device:TPU:2, one launch (start us, length us, event | category | flops | bytes accessed | tf_op | source)
XLA Modules:
  0.0 241.2 jit_solution(5012048735916774514)
XLA Ops:
  0.0 0.0 copy-start
  0.0 1.2 copy-done
  1.2 23.2 %fusion.4 = bf16[16,250,512]{2,1,0:T(8,128)(2,1)} fusion(bf16[16,250,1000]{2,0,1:T(8,128)(2,1)} %param.3, bf16[1000,512]{1,0:T(8,128)(2,1)S(1)} %copy-done), kind=kOutput, calls=%fused_computation.6 | convolution fusion | flops 4098048000 | bytes 13120000 | tf_op jit(solution)/shard_map/krs,sj->krj/dot_general | solution.py:8
  24.4 7.9 %copy.14 = bf16[16,250,512]{1,0,2:T(8,128)(2,1)} copy(bf16[16,250,512]{2,1,0:T(8,128)(2,1)} %fusion.4) | data formatting | bytes 8192000 | tf_op jit(solution)/shard_map/convert_element_type | solution.py:10
  32.3 55.3 %all_to_all.36 = bf16[16,250,512]{1,0,2:T(8,128)(2,1)} all-to-all(bf16[16,250,512]{1,0,2:T(8,128)(2,1)} %copy.14), channel_id=1, replica_groups=mesh['pair'=64,'mo'=4] {'mo'}, dimensions={2} | all-to-all | bytes 8192000 | tf_op jit(solution)/shard_map/all_to_all | solution.py:11
  87.7 8.5 %copy.16 = bf16[16,4,250,128]{3,0,2,1:T(8,128)(2,1)} copy(bf16[16,4,250,128]{2,0,3,1:T(8,128)(2,1)} %bitcast.18) | data formatting | bytes 8192000 | tf_op jit(solution)/shard_map/all_to_all | solution.py:11
  96.2 6.8 %fusion.7 = f32[16,512,128]{1,2,0:T(8,128)} fusion(bf16[16,1000,128]{2,0,1:T(8,128)(2,1)} %bitcast.17, bf16[1000,512]{1,0:T(8,128)(2,1)S(1)} %copy-done), kind=kOutput, calls=%fused_computation.7 | convolution fusion | flops 2097152000 | bytes 9314304 | tf_op jit(solution)/shard_map/ri,krj->kij/dot_general | solution.py:12
  103.1 5.5 %copy.18 = f32[16,512,128]{2,0,1:T(8,128)} copy(f32[16,512,128]{1,2,0:T(8,128)} %fusion.7) | data formatting | bytes 8388608 | tf_op jit(solution)/shard_map/ri,krj->kij/transpose | solution.py:12
  108.5 0.0 copy-start.1
  108.5 13.3 %all-to-all-start.1 = ((f32[16,512,128]{2,0,1:T(8,128)}), f32[16,512,128]{2,0,1:T(8,128)}, u32[]{:S(2)}, u32[]{:S(2)}) async-start(f32[16,512,128]{2,0,1:T(8,128)} %copy.18), calls=%async_computation.1 | async-start | bytes 8388608 | tf_op jit(solution)/shard_map/all_to_all | solution.py:13
  121.9 0.0 copy-done.1
  121.9 94.8 %all-to-all-done.1 = f32[16,512,128]{2,0,1:T(8,128)} async-done(((f32[16,512,128]{2,0,1:T(8,128)}), f32[16,512,128]{2,0,1:T(8,128)}, u32[]{:S(2)}, u32[]{:S(2)}) %all-to-all-start.1) | async-done | bytes 4194336 | tf_op jit(solution)/shard_map/all_to_all | solution.py:13
  216.8 6.1 %copy.20 = f32[64,16,8,128]{3,2,1,0:T(8,128)} copy(f32[64,16,8,128]{3,1,2,0:T(8,128)} %bitcast.8) | data formatting | bytes 8388608 | tf_op jit(solution)/shard_map/all_to_all | solution.py:13
  222.9 10.2 %gather_fusion = f32[1024,8,128]{2,1,0:T(8,128)} fusion(f32[1024,8,128]{2,1,0:T(8,128)} %bitcast.16, s32[1024]{0:T(1024)S(1)} %fusion.12), kind=kCustom, calls=%fused_computation | custom fusion | bytes 8392704 | tf_op jit(solution)/shard_map/jit(_take)/gather | solution.py:14
  233.1 8.1 %add_multiply_fusion = f32[1024,8,128]{2,1,0:T(8,128)} fusion(f32[1024,8,128]{2,1,0:T(8,128)} %gather_fusion, pred[1024]{0:T(1024)(128)(4,1)S(1)} %compare_and_fusion, f32[64,16,8,128]{3,2,1,0:T(8,128)} %copy.20), kind=kLoop, calls=%fused_computation.3 | loop fusion | flops 3145728 | bytes 12583936 | tf_op jit(solution)/shard_map/mul | solution.py:15
  (2 shorter events, 0.0 us)
Async XLA Ops:
  0.0 1.2 copy-start
  108.5 13.4 %copy-start.1 = (s32[1024]{0:T(1024)S(1)}, s32[1024]{0:T(1024)}, u32[]{:S(2)}) copy-start(s32[1024]{0:T(1024)} %param.5) | copy-start | bytes 12292
  108.5 108.2 %all-to-all-start.1 = ((f32[16,512,128]{2,0,1:T(8,128)}), f32[16,512,128]{2,0,1:T(8,128)}, u32[]{:S(2)}, u32[]{:S(2)}) async-start(f32[16,512,128]{2,0,1:T(8,128)} %copy.18), calls=%async_computation.1 | async-start | bytes 8388608 | tf_op jit(solution)/shard_map/all_to_all | solution.py:13
where the time goes:
time: 242 us; the launch traced here: 241 us
  waiting for transfers between devices  94.8 us (39%)
  blocking collectives  55.3 us (23%)
  local copies, waits for them, and re-layouts  39.5 us (16%)
  matrix products  30.1 us (12%)
  starting transfers between devices  13.3 us (5%)
  other arithmetic  8.1 us (3%)
    all_to_all x1, waiting for transfers between devices, on_device(): lax.all_to_all(half, 'pair', split_axis=1, concat_axis=0, tiled=True)  94.8 us
    all_to_all x1, blocking collectives, on_device(): lax.all_to_all(quarter, 'mo', split_axis=2, concat_axis=1, tiled=True)  55.3 us
    dot_general x1, matrix products, on_device(): jnp.einsum('krs,sj->krj', integrals, coeffs, preferred_element_type=jnp.f...  23.2 us
    all_to_all x1, starting transfers between devices, on_device(): lax.all_to_all(half, 'pair', split_axis=1, concat_axis=0, tiled=True)  13.3 us
    gather x1, local copies, waits for them, and re-layouts, on_device(): partner = jnp.take(pieces, mirror, axis=0)  10.2 us
    all_to_all x1, local copies, waits for them, and re-layouts, on_device(): lax.all_to_all(quarter, 'mo', split_axis=2, concat_axis=1, tiled=True)  8.54 us
    mul x1, other arithmetic, on_device(): return 0.5 * (pieces + partner)  8.09 us
    convert_element_type x1, local copies, waits for them, and re-layouts, on_device(): quarter = jnp.einsum('krs,sj->krj', integrals, coeffs, preferred_element_...  7.91 us
  transfers between devices with their start and end apart: 1, of which 1 were waited for; matrix products, arithmetic and copies ran while one was open for 0% of the time, Pallas kernels for 0%

commit v1 on v0

--- a/solution.py
+++ b/solution.py
@@ -8,7 +8,10 @@
     quarter = jnp.einsum(
         "krs,sj->krj", integrals, coeffs, preferred_element_type=jnp.float32
     ).astype(jnp.bfloat16)
-    arrived = lax.all_to_all(quarter, "mo", split_axis=2, concat_axis=1, tiled=True)
+    arrived = jnp.concatenate(
+        lax.all_to_all(jnp.stack(jnp.split(quarter, lax.axis_size("mo"), axis=2)), "mo", 0, 0),
+        axis=1,
+    )
     half = jnp.einsum("ri,krj->kij", coeffs, arrived, preferred_element_type=jnp.float32)
     pieces = lax.all_to_all(half, "pair", split_axis=1, concat_axis=0, tiled=True)
     partner = jnp.take(pieces, mirror, axis=0)

time: 242 us -> 223 us (0.921)
  local copies, waits for them, and re-layouts: 39.5 us -> 26.4 us
  matrix products: 30.1 us -> 26.6 us
    all_to_all x1 -> x0, local copies, waits for them, and re-layouts: 8.54 us -> none  [on_device(): lax.all_to_all(quarter, 'mo', split_axis=2, concat_axis=1, tiled=True)]
    convert_element_type x1 -> x0, local copies, waits for them, and re-layouts: 7.91 us -> none  [on_device(): quarter = jnp.einsum('krs,sj->krj', integrals, coeffs, preferred_element_...]
    another operation x0 -> x2, local copies, waits for them, and re-layouts: none -> 3.36 us  [on_device(): jnp.stack(jnp.split(quarter, lax.axis_size('mo'), axis=2))]
    all_to_all x1, blocking collectives: 55.3 us -> 52.9 us  [on_device(): lax.all_to_all(jnp.stack(jnp.split(quarter, lax.axis_size('mo'), axis=2))...]
where the time goes in v1:
time: 223 us
  waiting for transfers between devices  95.3 us (43%)
  blocking collectives  52.9 us (24%)
  matrix products  26.6 us (12%)
  local copies, waits for them, and re-layouts  26.4 us (12%)
  starting transfers between devices  12.5 us (6%)
  other arithmetic  8.87 us (4%)
    all_to_all x1, waiting for transfers between devices, on_device(): lax.all_to_all(half, 'pair', split_axis=1, concat_axis=0, tiled=True)  95.3 us
    all_to_all x1, blocking collectives, on_device(): lax.all_to_all(jnp.stack(jnp.split(quarter, lax.axis_size('mo'), axis=2))...  52.9 us
    dot_general x1, matrix products, on_device(): jnp.einsum('krs,sj->krj', integrals, coeffs, preferred_element_type=jnp.f...  21.9 us
    all_to_all x1, starting transfers between devices, on_device(): lax.all_to_all(half, 'pair', split_axis=1, concat_axis=0, tiled=True)  12.5 us
    gather x1, local copies, waits for them, and re-layouts, on_device(): partner = jnp.take(pieces, mirror, axis=0)  10.2 us
    mul x1, other arithmetic, on_device(): return 0.5 * (pieces + partner)  8.09 us
    all_to_all x1, local copies, waits for them, and re-layouts, on_device(): lax.all_to_all(half, 'pair', split_axis=1, concat_axis=0, tiled=True)  6.1 us
    transpose x1, local copies, waits for them, and re-layouts, on_device(): jnp.einsum('ri,krj->kij', coeffs, arrived, preferred_element_type=jnp.flo...  5.45 us
  transfers between devices with their start and end apart: 1, of which 1 were waited for; matrix products, arithmetic and copies ran while one was open for 0% of the time, Pallas kernels for 0%

profile of v1, /device:TPU:2, one launch (start us, length us, event | category | flops | bytes accessed | tf_op | source)
XLA Modules:
  0.0 222.5 jit_solution(9054487274622792626)
XLA Ops:
  0.0 0.0 copy-start
  0.0 1.2 copy-done
  1.2 21.9 %fusion.4 = bf16[16,250,512]{2,1,0:T(8,128)(2,1)S(1)} fusion(bf16[16,250,1000]{2,0,1:T(8,128)(2,1)} %param.3, bf16[1000,512]{1,0:T(8,128)(2,1)S(1)} %copy-done), kind=kOutput, calls=%fused_computation.7 | convolution fusion | flops 4098048000 | bytes 13120000 | tf_op jit(solution)/shard_map/krs,sj->krj/dot_general | solution.py:8
  23.1 0.7 slice_bitcast_fusion.3
  23.8 0.8 pad_maximum_fusion
  24.6 2.6 %copy.12 = bf16[4,16,250,128]{3,1,2,0:T(8,128)(2,1)S(1)} copy(bf16[4,16,250,128]{3,2,1,0:T(8,128)(2,1)S(1)} %pad_maximum_fusion) | data formatting | bytes 8192000 | tf_op jit(solution)/shard_map/stack | solution.py:12
  27.3 52.9 %all_to_all.23 = bf16[4,16,250,128]{3,1,2,0:T(8,128)(2,1)S(1)} all-to-all(bf16[4,16,250,128]{3,1,2,0:T(8,128)(2,1)S(1)} %copy.12), channel_id=1, replica_groups=mesh['pair'=64,'mo'=4] {'mo'}, dimensions={0} | all-to-all | bytes 8192000 | tf_op jit(solution)/shard_map/all_to_all | solution.py:12
  80.1 4.7 %fusion.7 = f32[16,512,128]{1,2,0:T(8,128)} fusion(bf16[16,1000,128]{2,0,1:T(8,128)(2,1)S(1)} %bitcast.24, bf16[1000,512]{1,0:T(8,128)(2,1)S(1)} %copy-done), kind=kOutput, calls=%fused_computation.8 | convolution fusion | flops 2097152000 | bytes 9314304 | tf_op jit(solution)/shard_map/ri,krj->kij/dot_general | solution.py:15
  84.8 5.5 %copy.14 = f32[16,512,128]{2,0,1:T(8,128)} copy(f32[16,512,128]{1,2,0:T(8,128)} %fusion.7) | data formatting | bytes 8388608 | tf_op jit(solution)/shard_map/ri,krj->kij/transpose | solution.py:15
  90.3 0.0 copy-start.1
  90.3 12.5 %all-to-all-start.1 = ((f32[16,512,128]{2,0,1:T(8,128)}), f32[16,512,128]{2,0,1:T(8,128)}, u32[]{:S(2)}, u32[]{:S(2)}) async-start(f32[16,512,128]{2,0,1:T(8,128)} %copy.14), calls=%async_computation.1 | async-start | bytes 8388608 | tf_op jit(solution)/shard_map/all_to_all | solution.py:16
  102.7 0.0 copy-done.1
  102.8 95.3 %all-to-all-done.1 = f32[16,512,128]{2,0,1:T(8,128)} async-done(((f32[16,512,128]{2,0,1:T(8,128)}), f32[16,512,128]{2,0,1:T(8,128)}, u32[]{:S(2)}, u32[]{:S(2)}) %all-to-all-start.1) | async-done | bytes 4194336 | tf_op jit(solution)/shard_map/all_to_all | solution.py:16
  198.1 6.1 %copy.16 = f32[64,16,8,128]{3,2,1,0:T(8,128)} copy(f32[64,16,8,128]{3,1,2,0:T(8,128)} %bitcast.10) | data formatting | bytes 8388608 | tf_op jit(solution)/shard_map/all_to_all | solution.py:16
  204.2 10.2 %gather_fusion = f32[1024,8,128]{2,1,0:T(8,128)} fusion(f32[1024,8,128]{2,1,0:T(8,128)} %bitcast.23, s32[1024]{0:T(1024)S(1)} %fusion.12), kind=kCustom, calls=%fused_computation | custom fusion | bytes 8392704 | tf_op jit(solution)/shard_map/jit(_take)/gather | solution.py:17
  214.4 8.1 %add_multiply_fusion = f32[1024,8,128]{2,1,0:T(8,128)} fusion(f32[1024,8,128]{2,1,0:T(8,128)} %gather_fusion, pred[1024]{0:T(1024)(128)(4,1)S(1)} %compare_and_fusion, f32[64,16,8,128]{3,2,1,0:T(8,128)} %copy.16), kind=kLoop, calls=%fused_computation.4 | loop fusion | flops 3145728 | bytes 12583936 | tf_op jit(solution)/shard_map/mul | solution.py:18
  (2 shorter events, 0.0 us)
Async XLA Ops:
  0.0 1.2 copy-start
  90.3 12.5 %copy-start.1 = (s32[1024]{0:T(1024)S(1)}, s32[1024]{0:T(1024)}, u32[]{:S(2)}) copy-start(s32[1024]{0:T(1024)} %param.5) | copy-start | bytes 12292
  90.3 107.8 %all-to-all-start.1 = ((f32[16,512,128]{2,0,1:T(8,128)}), f32[16,512,128]{2,0,1:T(8,128)}, u32[]{:S(2)}, u32[]{:S(2)}) async-start(f32[16,512,128]{2,0,1:T(8,128)} %copy.14), calls=%async_computation.1 | async-start | bytes 8388608 | tf_op jit(solution)/shard_map/all_to_all | solution.py:16
